TPU v7x, 32 devices: a whole 2x2x4 slice. The times are simulated.
32 devices in a mesh: dp: 8 (over y, x, core), tensor: 4 (over z).
Axes of the slice: x: 2, y: 2, z: 4, core: 2. Of those that a mesh axis runs over, the one named last changes fastest.
Arguments:
- tokens: bfloat16 [8192, 2048], P(('dp', 'tensor')), may hold values from -6 to 6
- lengths: int32 [8], P('dp'), may hold values from 513 to 1024, as said below
- routes: int32 [8192, 4], P('dp'), may hold values from 0 to 7, all different within a row; in each aligned block of 1024 rows (0 to 1023, 1024 to 2047, ...) at most 768 rows name the same one
- cotangent: bfloat16 [8192, 2048], P(('dp', 'tensor')), may hold values from -6 to 6
- norm_one: bfloat16 [2048], replicated, may hold values from 0.5 to 1.5
- qkv_weight: bfloat16 [2048, 3, 2048], P(None, None, 'tensor'), may hold values from -0.125 to 0.125
- qkv_bias: bfloat16 [3, 2048], P(None, 'tensor'), may hold values from -0.59765625 to 0.59765625
- out_weight: bfloat16 [2048, 2048], P('tensor'), may hold values from -1.5 to 1.5
- norm_two: bfloat16 [2048], replicated, may hold values from 0.5 to 1.5
- router_weight: bfloat16 [2048, 8], replicated, may hold values from -0.0625 to 0.0625
- expert_in: bfloat16 [8, 2048, 2, 1408], P(None, None, None, 'tensor'), may hold values from -0.125 to 0.125
- expert_out: bfloat16 [8, 1408, 2048], P(None, 'tensor'), may hold values from -0.625 to 0.625
- shared_in: bfloat16 [2048, 2, 5632], P(None, None, 'tensor'), may hold values from -0.125 to 0.125
- shared_out: bfloat16 [5632, 2048], P('tensor'), may hold values from -0.15625 to 0.15625
- shared_gate: bfloat16 [2048], replicated, may hold values from -0.125 to 0.125
Outputs:
- output: bfloat16 [8192, 2048], P(('dp', 'tensor'))
- input_grad: float32 [8192, 2048], P(('dp', 'tensor'))
- norm_one_grad: float32 [2048], replicated
- qkv_weight_grad: float32 [2048, 3, 2048], P('dp', None, 'tensor')
- qkv_bias_grad: float32 [3, 2048], P(None, 'tensor')
- out_weight_grad: float32 [2048, 2048], P('tensor', 'dp')
- norm_two_grad: float32 [2048], replicated
- router_grad: float32 [2048, 8], replicated
- expert_in_grad: float32 [8, 2048, 2, 1408], P(None, 'dp', None, 'tensor')
- expert_out_grad: float32 [8, 1408, 2048], P(None, 'tensor', 'dp')
- shared_in_grad: float32 [2048, 2, 5632], P('dp', None, 'tensor')
- shared_out_grad: float32 [5632, 2048], P('tensor', 'dp')
- shared_gate_grad: float32 [2048], replicated
Inputs may be any that keep to these rules, and one draw needn't show every extreme that they name: Row r holds one sequence in its first lengths[r] slots; the other slots are padding. In every draw some row is full. `routes`: the 4 experts of a slot are all different. Within each packed row (aligned blocks of 1024 slots) no expert is named more than 768 times; in some row some expert is named exactly 768 times.
All inputs are finite; a program needn't handle non-finite values.
Results may differ from a plain program's by a relative error of at most 0.018.
The roundings to bfloat16 on the way count: a program that leaves them out, or rounds other values in their place, can miss the bound.
Values may be sent and summed in bfloat16 or wider, within the bound.
A program may use at most 384 MiB of HBM per device.

v0:
```python
import jax
import jax.numpy as jnp
from jax import lax
from jax.sharding import PartitionSpec as P

HEAD_DIM = 128
epsilon = 1e-06
theta_base = 1000000.0
precise = lax.Precision.HIGHEST


def rotary_tables(row_count, head_width):
    half_index = jnp.arange(head_width // 2).astype(jnp.float32)
    frequency = theta_base ** (-2.0 * half_index / head_width)
    angles = jnp.arange(row_count).astype(jnp.float32)[:, None] * frequency[None, :]
    angles = jnp.concatenate([angles, angles], axis=-1)
    return (jnp.cos(angles)[:, None, :], jnp.sin(angles)[:, None, :])


def rotary(values, cos_table, sine_table):
    half_width = values.shape[-1] // 2
    turned = jnp.concatenate([-values[..., half_width:], values[..., :half_width]], axis=-1)
    return values * cos_table + turned * sine_table


def rotary_back(grads_in, cos_table, sine_table):
    half_width = grads_in.shape[-1] // 2
    scaled = grads_in * sine_table
    return grads_in * cos_table + jnp.concatenate(
        [scaled[..., half_width:], -scaled[..., :half_width]], axis=-1
    )


def swiglu_back(gate_up, d_inner):
    gate_part = gate_up[:, 0]
    up_part = gate_up[:, 1]
    gate_sig = jax.nn.sigmoid(gate_part)
    d_gate = d_inner * up_part * gate_sig * (1.0 + gate_part * (1.0 - gate_sig))
    d_up = d_inner * gate_part * gate_sig
    return jnp.stack([d_gate, d_up], axis=1)


def norm_back(d_normed, unit_rows, inverse, gain_vector):
    d_unit = d_normed * gain_vector
    return inverse * (d_unit - unit_rows * jnp.mean(d_unit * unit_rows, axis=-1, keepdims=True))


def expert_forward(row_data, in_weight, down_weight):
    in_flat = in_weight.reshape(in_weight.shape[0], -1)
    gate_up = jnp.dot(row_data, in_flat, preferred_element_type=jnp.float32).reshape(
        row_data.shape[0], 2, -1
    )
    inner_act = (jax.nn.silu(gate_up[:, 0]) * gate_up[:, 1]).astype(jnp.bfloat16)
    result = jnp.dot(inner_act, down_weight, preferred_element_type=jnp.float32)
    return (gate_up, inner_act, result)


def expert_backward(row_data, d_rows, scale_rows, gate_up, inner_act, in_weight, down_weight):
    d_result = (scale_rows[:, None] * d_rows).astype(jnp.bfloat16)
    down_grad = jnp.einsum("nf,nd->fd", inner_act, d_result, preferred_element_type=jnp.float32)
    d_inner = jnp.einsum("nd,fd->nf", d_result, down_weight, preferred_element_type=jnp.float32)
    projected = jnp.einsum("nd,fd->nf", d_rows, down_weight, preferred_element_type=jnp.float32)
    d_scale = jnp.sum(projected * inner_act.astype(jnp.float32), axis=-1)
    d_gate_up = swiglu_back(gate_up, d_inner).reshape(row_data.shape[0], -1).astype(jnp.bfloat16)
    in_flat = in_weight.reshape(in_weight.shape[0], -1)
    in_grad = jnp.einsum("nd,nc->dc", row_data, d_gate_up, preferred_element_type=jnp.float32)
    d_rows_in = jnp.einsum("nc,dc->nd", d_gate_up, in_flat, preferred_element_type=jnp.float32)
    return (in_grad.reshape(in_weight.shape), down_grad, d_scale, d_rows_in)


def on_device(
    tokens,
    lengths,
    routes,
    cotangent,
    norm_one,
    qkv_weight,
    qkv_bias,
    out_weight,
    norm_two,
    router_weight,
    expert_in,
    expert_out,
    shared_in,
    shared_out,
    shared_gate,
):
    own_rows = tokens.shape[0]
    slot_count = routes.shape[0]
    model_width = tokens.shape[1]
    qkv_cols = qkv_weight.shape[2]
    local_heads = qkv_cols // HEAD_DIM
    experts_total = router_weight.shape[1]
    length = lengths[0]
    tensor_index = lax.axis_index("tensor")
    first_row = tensor_index * own_rows
    slot_index = jnp.arange(slot_count)
    live_own = (first_row + jnp.arange(own_rows) < length).astype(jnp.float32)[:, None]
    block_rows = min(512, slot_count)
    scale = HEAD_DIM ** (-0.5)
    tokens_f = tokens.astype(jnp.float32)
    gain_one = norm_one.astype(jnp.float32)
    gain_two = norm_two.astype(jnp.float32)
    inv_one = lax.rsqrt(jnp.mean(tokens_f * tokens_f, axis=-1, keepdims=True) + epsilon)
    unit_one = tokens_f * inv_one
    normed_one = lax.all_gather(
        (unit_one * gain_one).astype(jnp.bfloat16), "tensor", axis=0, tiled=True
    )
    qkv_flat_weight = qkv_weight.reshape(model_width, 3 * qkv_cols)
    qkv_all = jnp.dot(normed_one, qkv_flat_weight, preferred_element_type=jnp.float32)
    qkv_all = qkv_all.reshape(slot_count, 3, qkv_cols) + qkv_bias.astype(jnp.float32)
    cos_table, sine_table = rotary_tables(slot_count, HEAD_DIM)
    query_heads = rotary(
        qkv_all[:, 0].reshape(slot_count, local_heads, HEAD_DIM), cos_table, sine_table
    ).astype(jnp.bfloat16)
    key_heads = rotary(
        qkv_all[:, 1].reshape(slot_count, local_heads, HEAD_DIM), cos_table, sine_table
    ).astype(jnp.bfloat16)
    value_heads = qkv_all[:, 2].reshape(slot_count, local_heads, HEAD_DIM).astype(jnp.bfloat16)

    def block_scores(block_start, block_end):
        raw_scores = (
            jnp.einsum(
                "qhd,khd->hqk",
                query_heads[block_start:block_end],
                key_heads[:block_end],
                preferred_element_type=jnp.float32,
            )
            * scale
        )
        allowed = (slot_index[None, :block_end] <= slot_index[block_start:block_end, None]) & (
            slot_index[None, :block_end] < length
        )
        return jnp.where(allowed[None], raw_scores, -1000000000.0)

    mixed_parts = []
    lse_parts = []
    for block_start in range(0, slot_count, block_rows):
        block_end = block_start + block_rows
        raw_scores = block_scores(block_start, block_end)
        row_peak = jnp.max(raw_scores, axis=-1, keepdims=True)
        exp_terms = jnp.exp(raw_scores - row_peak)
        summed = jnp.sum(exp_terms, axis=-1, keepdims=True)
        probs_low = (exp_terms / summed).astype(jnp.bfloat16)
        mixed_parts.append(
            jnp.einsum(
                "hqk,khd->qhd",
                probs_low,
                value_heads[:block_end],
                preferred_element_type=jnp.float32,
            )
        )
        lse_parts.append(row_peak + jnp.log(summed))
    mixed = jnp.concatenate(mixed_parts, axis=0).reshape(slot_count, qkv_cols).astype(jnp.bfloat16)
    branch_one = lax.psum_scatter(
        jnp.dot(mixed, out_weight, preferred_element_type=jnp.float32),
        "tensor",
        scatter_dimension=0,
        tiled=True,
    )
    hidden = tokens_f + live_own * branch_one
    inv_two = lax.rsqrt(jnp.mean(hidden * hidden, axis=-1, keepdims=True) + epsilon)
    unit_two = hidden * inv_two
    normed_two = lax.all_gather(
        (unit_two * gain_two).astype(jnp.bfloat16), "tensor", axis=0, tiled=True
    )
    router_probs = jax.nn.softmax(
        jnp.dot(normed_two, router_weight, preferred_element_type=jnp.float32), axis=-1
    )
    picked = jnp.sum(
        (routes[:, :, None] == jnp.arange(experts_total)[None, None, :]).astype(jnp.float32), axis=1
    )
    weights = router_probs * picked
    combined = jnp.zeros((slot_count, model_width), jnp.float32)
    kept_rows = []
    for expert in range(experts_total):
        gate_up, inner_act, result = expert_forward(
            normed_two, expert_in[expert], expert_out[expert]
        )
        combined = combined + weights[:, expert : expert + 1] * result
        kept_rows.append((gate_up, inner_act))
    shared_up, shared_act, shared_result = expert_forward(normed_two, shared_in, shared_out)
    gate_value = jax.nn.sigmoid(
        jnp.dot(normed_two, shared_gate, preferred_element_type=jnp.float32)
    )
    combined = combined + gate_value[:, None] * shared_result
    branch_two = lax.psum_scatter(
        combined.astype(jnp.bfloat16), "tensor", scatter_dimension=0, tiled=True
    ).astype(jnp.float32)
    output = (hidden + live_own * branch_two).astype(jnp.bfloat16)
    grad_out = cotangent.astype(jnp.float32) * live_own
    d_two = lax.all_gather((live_own * grad_out).astype(jnp.bfloat16), "tensor", axis=0, tiled=True)
    shared_in_grad, shared_out_grad, d_shared_scale, d_normed = expert_backward(
        normed_two, d_two, gate_value, shared_up, shared_act, shared_in, shared_out
    )
    d_gate_logit = d_shared_scale * gate_value * (1.0 - gate_value)
    in_grads = []
    out_grads = []
    d_columns = []
    for expert in range(experts_total):
        gate_up, inner_act = kept_rows[expert]
        in_grad, down_grad, d_scale, d_rows_in = expert_backward(
            normed_two,
            d_two,
            weights[:, expert],
            gate_up,
            inner_act,
            expert_in[expert],
            expert_out[expert],
        )
        d_normed = d_normed + d_rows_in
        d_columns.append(d_scale)
        in_grads.append(in_grad)
        out_grads.append(down_grad)
    expert_in_grad = jnp.stack(in_grads, axis=0)
    expert_out_grad = jnp.stack(out_grads, axis=0)
    d_probs = jnp.stack(d_columns, axis=1) * picked
    d_logits = router_probs * (d_probs - jnp.sum(router_probs * d_probs, axis=-1, keepdims=True))
    d_normed = d_normed + jnp.einsum(
        "se,de->sd", d_logits, router_weight.astype(jnp.float32), precision=precise
    )
    d_normed = d_normed + d_gate_logit[:, None] * shared_gate.astype(jnp.float32)[None, :]
    small_cols = jnp.concatenate([d_logits, d_gate_logit[:, None]], axis=1)
    col_sums = jnp.einsum(
        "sc,sd->cd", small_cols, normed_two.astype(jnp.float32), precision=precise
    )
    router_part = col_sums[:experts_total].T
    gate_part = col_sums[experts_total]
    grad_two = lax.psum_scatter(d_normed, "tensor", scatter_dimension=0, tiled=True)
    norm_two_part = jnp.sum(grad_two * unit_two, axis=0)
    grad_hidden = grad_out + norm_back(grad_two, unit_two, inv_two, gain_two)
    d_one = lax.all_gather(
        (live_own * grad_hidden).astype(jnp.bfloat16), "tensor", axis=0, tiled=True
    )
    out_weight_grad = jnp.einsum("sc,sd->cd", mixed, d_one, preferred_element_type=jnp.float32)
    d_mixed = jnp.einsum("sd,cd->sc", d_one, out_weight, preferred_element_type=jnp.float32)
    d_mixed = d_mixed.astype(jnp.bfloat16).reshape(slot_count, local_heads, HEAD_DIM)
    d_query_parts = []
    d_key = jnp.zeros((slot_count, local_heads, HEAD_DIM), jnp.float32)
    d_value = jnp.zeros((slot_count, local_heads, HEAD_DIM), jnp.float32)
    for block_number, block_start in enumerate(range(0, slot_count, block_rows)):
        block_end = block_start + block_rows
        raw_scores = block_scores(block_start, block_end)
        probs_full = jnp.exp(raw_scores - lse_parts[block_number])
        probs_low = probs_full.astype(jnp.bfloat16)
        d_grad_block = d_mixed[block_start:block_end]
        d_probs_att = jnp.einsum(
            "qhd,khd->hqk",
            d_grad_block,
            value_heads[:block_end],
            preferred_element_type=jnp.float32,
        )
        delta_sum = jnp.sum(probs_full * d_probs_att, axis=-1, keepdims=True)
        d_scores = (probs_full * (d_probs_att - delta_sum)).astype(jnp.bfloat16)
        d_query_parts.append(
            jnp.einsum(
                "hqk,khd->qhd", d_scores, key_heads[:block_end], preferred_element_type=jnp.float32
            )
            * scale
        )
        d_key = d_key.at[:block_end].add(
            jnp.einsum(
                "hqk,qhd->khd",
                d_scores,
                query_heads[block_start:block_end],
                preferred_element_type=jnp.float32,
            )
            * scale
        )
        d_value = d_value.at[:block_end].add(
            jnp.einsum("hqk,qhd->khd", probs_low, d_grad_block, preferred_element_type=jnp.float32)
        )
    d_query = jnp.concatenate(d_query_parts, axis=0)
    d_qkv = jnp.stack(
        [
            rotary_back(d_query, cos_table, sine_table).reshape(slot_count, qkv_cols),
            rotary_back(d_key, cos_table, sine_table).reshape(slot_count, qkv_cols),
            d_value.reshape(slot_count, qkv_cols),
        ],
        axis=1,
    ).astype(jnp.bfloat16)
    d_qkv_flat = d_qkv.reshape(slot_count, 3 * qkv_cols)
    qkv_weight_grad = jnp.einsum(
        "sd,sc->dc", normed_one, d_qkv_flat, preferred_element_type=jnp.float32
    )
    qkv_weight_grad = qkv_weight_grad.reshape(model_width, 3, qkv_cols)
    bias_part = jnp.sum(d_qkv.astype(jnp.float32), axis=0)
    grad_one = jnp.einsum(
        "sc,dc->sd", d_qkv_flat, qkv_flat_weight, preferred_element_type=jnp.float32
    )
    grad_one = lax.psum_scatter(
        grad_one.astype(jnp.bfloat16), "tensor", scatter_dimension=0, tiled=True
    ).astype(jnp.float32)
    norm_one_part = jnp.sum(grad_one * unit_one, axis=0)
    input_grad = grad_hidden + norm_back(grad_one, unit_one, inv_one, gain_one)
    column_start = tensor_index * qkv_cols
    zero_index = jnp.zeros((), jnp.int32)
    bias_full = lax.dynamic_update_slice(
        jnp.zeros((3, qkv_cols * lax.axis_size("tensor")), jnp.float32),
        bias_part,
        (zero_index, column_start),
    )
    norm_one_grad, norm_two_grad, router_grad, shared_gate_grad, bias_sum = lax.psum(
        (norm_one_part, norm_two_part, router_part, gate_part, bias_full), ("dp", "tensor")
    )
    qkv_bias_grad = lax.dynamic_slice(bias_sum, (zero_index, column_start), (3, qkv_cols))
    qkv_sum, out_sum, expert_in_sum, expert_out_sum, shared_in_sum, shared_out_sum = (
        lax.psum_scatter(
            qkv_weight_grad.astype(jnp.bfloat16), "dp", scatter_dimension=0, tiled=True
        ).astype(jnp.float32),
        lax.psum_scatter(
            out_weight_grad.astype(jnp.bfloat16), "dp", scatter_dimension=1, tiled=True
        ).astype(jnp.float32),
        lax.psum_scatter(
            expert_in_grad.astype(jnp.bfloat16), "dp", scatter_dimension=1, tiled=True
        ).astype(jnp.float32),
        lax.psum_scatter(
            expert_out_grad.astype(jnp.bfloat16), "dp", scatter_dimension=2, tiled=True
        ).astype(jnp.float32),
        lax.psum_scatter(
            shared_in_grad.astype(jnp.bfloat16), "dp", scatter_dimension=0, tiled=True
        ).astype(jnp.float32),
        lax.psum_scatter(
            shared_out_grad.astype(jnp.bfloat16), "dp", scatter_dimension=1, tiled=True
        ).astype(jnp.float32),
    )
    return (
        output,
        input_grad,
        norm_one_grad,
        qkv_sum,
        qkv_bias_grad,
        out_sum,
        norm_two_grad,
        router_grad,
        expert_in_sum,
        expert_out_sum,
        shared_in_sum,
        shared_out_sum,
        shared_gate_grad,
    )


def solution(mesh):
    in_specs = (
        P(("dp", "tensor"), None),
        P("dp"),
        P("dp", None),
        P(("dp", "tensor"), None),
        P(),
        P(None, None, "tensor"),
        P(None, "tensor"),
        P("tensor", None),
        P(),
        P(),
        P(None, None, None, "tensor"),
        P(None, "tensor", None),
        P(None, None, "tensor"),
        P("tensor", None),
        P(),
    )
    out_specs = (
        P(("dp", "tensor"), None),
        P(("dp", "tensor"), None),
        P(),
        P("dp", None, "tensor"),
        P(None, "tensor"),
        P("tensor", "dp"),
        P(),
        P(),
        P(None, "dp", None, "tensor"),
        P(None, "tensor", "dp"),
        P("dp", None, "tensor"),
        P("tensor", "dp"),
        P(),
    )
    return jax.shard_map(
        on_device, mesh=mesh, in_specs=in_specs, out_specs=out_specs, check_vma=False
    )
```

profile of v0, /device:TPU:1, one launch (start us, length us, event | category | flops | bytes accessed | tf_op | source)
XLA Modules:
  0.0 1673.9 jit_solution(9152987854078074397)
XLA Ops:
  26.3 69.4 %all-gather.5.cloned.1.call-done = bf16[1024,2048]{1,0:T(8,128)(2,1)} async-done(((bf16[256,2048]{1,0:T(8,128)(2,1)}), bf16[1024,2048]{1,0:T(8,128)(2,1)}) %all-gather.5.cloned.1.call-update) | async-done | bytes 4194320 | tf_op jit(solution)/shard_map/all_gather | solution.py:106
  140.0 142.3 %reduce-scatter.11.cloned.1.call-done = f32[256,2048]{1,0:T(8,128)} async-done(((f32[1024,2048]{1,0:T(8,128)}), f32[256,2048]{1,0:T(8,128)}) %reduce-scatter.11.cloned.1.call-update) | async-done | bytes 2097168 | tf_op jit(solution)/shard_map/reduce_scatter | solution.py:155
  289.6 11.4 copy.161
  301.1 15.1 copy.107
  316.8 16.4 fusion.447
  333.3 36.9 %all-gather.7.cloned.1.call-done = bf16[1024,2048]{1,0:T(8,128)(2,1)} async-done(((bf16[256,2048]{1,0:T(8,128)(2,1)}), bf16[1024,2048]{1,0:T(8,128)(2,1)}) %all-gather.7.cloned.1.call-update) | async-done | bytes 4194320 | tf_op jit(solution)/shard_map/all_gather | solution.py:164
  417.0 34.5 %all-gather.9.cloned.1.call-done = bf16[1024,2048]{1,0:T(8,128)(2,1)} async-done(((bf16[256,2048]{1,0:T(8,128)(2,1)}), bf16[1024,2048]{1,0:T(8,128)(2,1)}) %all-gather.9.cloned.1.call-update) | async-done | bytes 4194320 | tf_op jit(solution)/shard_map/all_gather | solution.py:192
  471.8 17.7 %fusion.46 = f32[1024,2,1408]{2,0,1:T(8,128)S(1)} fusion(bf16[2,1408,2048]{2,1,0:T(8,128)(2,1)} %bitcast.918, bf16[1024,2048]{1,0:T(8,128)(2,1)} %all-gather.7.cloned.1.call-done), kind=kOutput, calls=%fused_computation.74 | convolution fusion | flops 11811160064 | bytes 27262976 | tf_op jit(solution)/shard_map/dot_general | solution.py:50
  595.8 12.7 multiply_bitcast_fusion.1
  608.5 38.0 %fusion.19 = f32[1024,2048]{1,0:T(8,128)} fusion(f32[1024,2048]{1,0:T(8,128)} %fusion.501, f32[1024,2048]{1,0:T(8,128)} %fusion.500, f32[1024,2048]{1,0:T(8,128)} %fusion.499, f32[1024,2048]{1,0:T(8,128)} %fusion.498, f32[1024,2048]{1,0:T(8,128)} %fusion.497, f32[1024,2048]{1,0:T(8,128)} %fusion.496, f32[1024,2048]{1,0:T(8,128)} %fusion.495, ...), kind=kOutput, calls=%fused_computation.32 | convolution fusion | flops 11837112320 | bytes 101199872 | tf_op jit(solution)/shard_map/nc,dc->nd/dot_general | solution.py:67
  697.5 29.5 %add_convert_fusion = bf16[1024,2048]{1,0:T(8,128)(2,1)} fusion(f32[1024,2048]{1,0:T(8,128)} %fusion.319, f32[1024,2048]{1,0:T(8,128)} %fusion.323, f32[1024,2048]{1,0:T(8,128)} %fusion.327, f32[1024,2048]{1,0:T(8,128)} %fusion.331, f32[1024,2048]{1,0:T(8,128)} %fusion.335, f32[1024,2048]{1,0:T(8,128)} %fusion.339, f32[1024,2048]{1,0:T(8,128)} %fusion.343, ...), kind=kOutput, calls=%fused_computation.36 | convolution fusion | flops 5943328768 | bytes 79990784 | tf_op jit(solution)/shard_map/dot_general | solution.py:54
  727.1 62.4 %reduce-scatter.15.cloned.1.call-done = f32[256,2048]{1,0:T(8,128)} async-done(((f32[1024,2048]{1,0:T(8,128)}), f32[256,2048]{1,0:T(8,128)}) %reduce-scatter.15.cloned.1.call-update) | async-done | bytes 2097168 | tf_op jit(solution)/shard_map/reduce_scatter | solution.py:229
  792.9 77.0 %reduce-scatter.13.cloned.1.call-done = bf16[256,2048]{1,0:T(8,128)(2,1)} async-done(((bf16[1024,2048]{1,0:T(8,128)(2,1)}), bf16[256,2048]{1,0:T(8,128)(2,1)}) %reduce-scatter.13.cloned.1.call-update) | async-done | bytes 1048592 | tf_op jit(solution)/shard_map/reduce_scatter | solution.py:187
  875.8 10.7 convolution_convert_fusion.1
  928.6 19.2 %convolution_convert_fusion = bf16[2048,2,1408]{2,0,1:T(8,128)(2,1)} fusion(bf16[1024,2,1408]{0,2,1:T(8,128)(2,1)} %copy.137, bf16[1024,2048]{1,0:T(8,128)(2,1)} %all-gather.7.cloned.1.call-done), kind=kOutput, calls=%fused_computation.12 | convolution fusion | flops 11816927232 | bytes 21495808 | tf_op jit(solution)/shard_map/nd,nc->dc/dot_general | solution.py:66
  1028.5 12.0 bitcast_convert_fusion
  1045.3 11.5 convolution_convert_fusion.2
  1112.1 86.9 %reduce-scatter.27.cloned.1.call-done = bf16[256,2,1408]{2,0,1:T(8,128)(2,1)} async-done(((bf16[2048,2,1408]{2,0,1:T(8,128)(2,1)}), bf16[256,2,1408]{2,0,1:T(8,128)(2,1)}) %reduce-scatter.27.cloned.1.call-update) | async-done | bytes 1441808 | tf_op jit(solution)/shard_map/reduce_scatter | solution.py:320
  1203.5 40.1 %reduce-scatter.21.cloned.1.call-done = bf16[512,256]{1,0:T(8,128)(2,1)} async-done(((bf16[512,2048]{1,0:T(8,128)(2,1)}), bf16[512,256]{1,0:T(8,128)(2,1)}) %reduce-scatter.21.cloned.1.call-update) | async-done | bytes 262160 | tf_op jit(solution)/shard_map/reduce_scatter | solution.py:311
  1245.4 77.9 %reduce-scatter.17.cloned.1.call-done = bf16[256,2048]{1,0:T(8,128)(2,1)} async-done(((bf16[1024,2048]{1,0:T(8,128)(2,1)}), bf16[256,2048]{1,0:T(8,128)(2,1)}) %reduce-scatter.17.cloned.1.call-update) | async-done | bytes 1048592 | tf_op jit(solution)/shard_map/reduce_scatter | solution.py:291
  1325.4 42.1 %all-reduce.2 = (f32[2048]{0:T(1024)}, f32[3,2048]{1,0:T(4,128)S(1)}, f32[2048]{0:T(1024)}, f32[2048]{0:T(1024)}) all-reduce(f32[2048]{0:T(1024)S(1)} %get-tuple-element.118, f32[3,2048]{1,0:T(4,128)S(1)} %constant_dynamic-update-slice_fusion, f32[2048]{0:T(1024)S(1)} %copy-done.152, ...), channel_id=1, replica_groups=mesh['dp'=8,'tensor'=4] {'dp','tensor'}, use_global_device_ids=true, to_apply=%region_28.29 | all-reduce | flops 12288 | bytes 98304 | tf_op jit(solution)/shard_map/psum | solution.py:303
  1371.9 17.6 %reduce-scatter.19.cloned.1.call-done = bf16[256,3,512]{2,0,1:T(8,128)(2,1)} async-done(((bf16[2048,3,512]{2,0,1:T(8,128)(2,1)}), bf16[256,3,512]{2,0,1:T(8,128)(2,1)}) %reduce-scatter.19.cloned.1.call-update) | async-done | bytes 786448 | tf_op jit(solution)/shard_map/reduce_scatter | solution.py:308
  1392.0 147.4 %reduce-scatter.23.cloned.1.call-done = bf16[8,256,2,352]{1,3,2,0:T(8,128)(2,1)} async-done(((bf16[8,2048,2,352]{1,3,2,0:T(8,128)(2,1)}), bf16[8,256,2,352]{1,3,2,0:T(8,128)(2,1)}) %reduce-scatter.23.cloned.1.call-update) | async-done | bytes 2883600 | tf_op jit(solution)/shard_map/reduce_scatter | solution.py:314
  1544.4 121.3 %all-reduce.5.cloned.1.call-done = f32[2048,8]{0,1:T(8,128)} async-done(((f32[2048,8]{0,1:T(8,128)}), f32[2048,8]{0,1:T(8,128)}) %all-reduce.5.cloned.1.call-update) | async-done | bytes 65552 | tf_op jit(solution)/shard_map/psum | solution.py:303
  (604 shorter events, 506.5 us)
Async XLA Ops:
  7.2 88.5 %all-gather.5.cloned.1.call-start = ((), (), s32[]{:S(2)}) async-start(), calls=%async_computation.10 | async-start | bytes 5242880 | tf_op jit(solution)/shard_map/all_gather | solution.py:106
  12.7 269.6 %reduce-scatter.11.cloned.1.call-start = ((), (), s32[]{:S(2)}) async-start(), calls=%async_computation.11 | async-start | bytes 10485760 | tf_op jit(solution)/shard_map/reduce_scatter | solution.py:155
  139.3 143.0 %copy-start.10 = (bf16[256,2048]{1,0:T(8,128)(2,1)S(1)}, bf16[256,2048]{1,0:T(8,128)(2,1)}, u32[]{:S(2)}) copy-start(bf16[256,2048]{1,0:T(8,128)(2,1)} %param.27) | copy-start | bytes 3145732
  139.3 230.9 %all-gather.7.cloned.1.call-start = ((), (), s32[]{:S(2)}) async-start(), calls=%async_computation.12 | async-start | bytes 5242880 | tf_op jit(solution)/shard_map/all_gather | solution.py:164
  140.0 145.9 %copy-start.129 = (f32[2048]{0:T(1024)}, f32[2048]{0:T(1024)S(1)}, u32[]{:S(2)}) copy-start(f32[2048]{0:T(1024)S(1)} %convert_element_type.408) | copy-start | bytes 24580
  140.0 145.8 %copy-start.164 = (f32[256]{0:T(256)}, f32[256]{0:T(256)S(1)}, u32[]{:S(2)}) copy-start(f32[256]{0:T(256)S(1)} %compare_convert_fusion) | copy-start | bytes 3076
  288.4 163.2 %all-gather.9.cloned.1.call-start = ((), (), s32[]{:S(2)}) async-start(), calls=%async_computation.14 | async-start | bytes 5242880 | tf_op jit(solution)/shard_map/all_gather | solution.py:192
  333.2 456.3 %reduce-scatter.15.cloned.1.call-start = ((), (), s32[]{:S(2)}) async-start(), calls=%async_computation.15 | async-start | bytes 10485760 | tf_op jit(solution)/shard_map/reduce_scatter | solution.py:229
  646.5 223.4 %reduce-scatter.13.cloned.1.call-start = ((), (), s32[]{:S(2)}) async-start(), calls=%async_computation.13 | async-start | bytes 5242880 | tf_op jit(solution)/shard_map/reduce_scatter | solution.py:187
  727.0 142.9 %copy-start.28 = (bf16[256,2048]{1,0:T(8,128)(2,1)S(1)}, bf16[256,2048]{1,0:T(8,128)(2,1)}, u32[]{:S(2)}) copy-start(bf16[256,2048]{1,0:T(8,128)(2,1)} %param.30) | copy-start | bytes 3145732
  727.0 142.9 %copy-start.165 = (f32[256]{0:T(256)S(1)}, f32[256]{0:T(256)}, u32[]{:S(2)}) copy-start(f32[256]{0:T(256)} %copy-done.164) | copy-start | bytes 3076
  727.0 230.1 %all-gather.11.cloned.1.call-start = ((), (), s32[]{:S(2)}) async-start(), calls=%async_computation.16 | async-start | bytes 5242880 | tf_op jit(solution)/shard_map/all_gather | solution.py:232
  875.8 226.7 %reduce-scatter.29.cloned.1.call-start = ((), (), s32[]{:S(2)}) async-start(), calls=%async_computation.24 | async-start | bytes 6488064 | tf_op jit(solution)/shard_map/reduce_scatter | solution.py:323
  886.6 222.3 %reduce-scatter.25.cloned.1.call-start = ((), (), s32[]{:S(2)}) async-start(), calls=%async_computation.22 | async-start | bytes 12976128 | tf_op jit(solution)/shard_map/reduce_scatter | solution.py:317
  913.9 285.2 %reduce-scatter.27.cloned.1.call-start = ((), (), s32[]{:S(2)}) async-start(), calls=%async_computation.23 | async-start | bytes 12976128 | tf_op jit(solution)/shard_map/reduce_scatter | solution.py:320
  947.8 295.8 %reduce-scatter.21.cloned.1.call-start = ((), (), s32[]{:S(2)}) async-start(), calls=%async_computation.19 | async-start | bytes 2359296 | tf_op jit(solution)/shard_map/reduce_scatter | solution.py:311
  989.0 334.3 %reduce-scatter.17.cloned.1.call-start = ((), (), s32[]{:S(2)}) async-start(), calls=%async_computation.17 | async-start | bytes 5242880 | tf_op jit(solution)/shard_map/reduce_scatter | solution.py:291
  1040.6 349.0 %reduce-scatter.19.cloned.1.call-start = ((), (), s32[]{:S(2)}) async-start(), calls=%async_computation.18 | async-start | bytes 7077888 | tf_op jit(solution)/shard_map/reduce_scatter | solution.py:308
  1056.9 482.5 %reduce-scatter.23.cloned.1.call-start = ((), (), s32[]{:S(2)}) async-start(), calls=%async_computation.21 | async-start | bytes 25952256 | tf_op jit(solution)/shard_map/reduce_scatter | solution.py:314
  1097.1 568.6 %all-reduce.5.cloned.1.call-start = ((), (), s32[]{:S(2)}) async-start(), calls=%async_computation.20 | async-start | bytes 131072 | tf_op jit(solution)/shard_map/psum | solution.py:303
  1112.1 211.2 %copy-start.11 = (bf16[256,2048]{1,0:T(8,128)(2,1)S(1)}, bf16[256,2048]{1,0:T(8,128)(2,1)}, u32[]{:S(2)}) copy-start(bf16[256,2048]{1,0:T(8,128)(2,1)} %param.27) | copy-start | bytes 3145732
  1112.1 211.2 %copy-start.127 = (f32[2048]{0:T(1024)S(1)}, f32[2048]{0:T(1024)}, u32[]{:S(2)}) copy-start(f32[2048]{0:T(1024)} %copy-done.126) | copy-start | bytes 24580
  1112.1 211.2 %copy-start.157 = (f32[256]{0:T(256)S(1)}, f32[256]{0:T(256)}, u32[]{:S(2)}) copy-start(f32[256]{0:T(256)} %copy-done.156) | copy-start | bytes 3076
  1112.1 213.2 %copy-start.152 = (f32[2048]{0:T(1024)S(1)}, f32[2048]{0:T(1024)}, u32[]{:S(2)}) copy-start(f32[2048]{0:T(1024)} %get-tuple-element.116) | copy-start | bytes 24580
  (184 other events, 2078.9 us)
Sparse Core Ops, SparseCore 0:
  12.8 82.8 all-gather.4
  139.4 142.8 reduce-scatter.10
  288.5 81.6 all-gather.6
  372.2 79.2 all-gather.8
  646.7 142.8 reduce-scatter.14
  792.2 77.6 reduce-scatter.12
  875.9 81.2 all-gather.10
  961.0 57.5 reduce-scatter.28
  1022.1 86.7 reduce-scatter.24
  1112.2 86.7 reduce-scatter.26
  1202.4 41.2 reduce-scatter.20
  1246.4 76.8 reduce-scatter.16
  1326.7 62.8 reduce-scatter.18
  1393.4 145.9 reduce-scatter.22
  1546.3 119.2 all-reduce.4
where the time goes:
time: 1680 us; the launch traced here: 1670 us
  waiting for transfers between devices  922 us (55%)
  matrix products  451 us (27%)
  local copies, waits for them, and re-layouts  148 us (9%)
  other arithmetic  92.2 us (5%)
  blocking collectives  42.1 us (3%)
  between operations  17.1 us (1%)
    reduce_scatter x1, waiting for transfers between devices, on_device(): lax.psum_scatter(expert_in_grad.astype(jnp.bfloat16), 'dp', scatter_dimen...  147 us
    reduce_scatter x1, waiting for transfers between devices, on_device(): lax.psum_scatter(jnp.dot(mixed, out_weight, preferred_element_type=jnp.fl...  142 us
    psum x1, waiting for transfers between devices, on_device(): lax.psum((norm_one_part, norm_two_part, router_part, gate_part, bias_full...  121 us
    reduce_scatter x1, waiting for transfers between devices, on_device(): lax.psum_scatter(shared_in_grad.astype(jnp.bfloat16), 'dp', scatter_dimen...  86.9 us
    dot_general x9, matrix products, expert_backward(): jnp.einsum('nc,dc->nd', d_gate_up, in_flat, preferred_element_type=jnp.fl...  83.9 us
    dot_general x9, matrix products, expert_forward(): result = jnp.dot(inner_act, down_weight, preferred_element_type=jnp.float32)  79.8 us
    reduce_scatter x1, waiting for transfers between devices, on_device(): lax.psum_scatter(grad_one.astype(jnp.bfloat16), 'tensor', scatter_dimensi...  77.9 us
    reduce_scatter x1, waiting for transfers between devices, on_device(): lax.psum_scatter(combined.astype(jnp.bfloat16), 'tensor', scatter_dimensi...  77 us
  transfers between devices with their start and end apart: 15, of which 14 were waited for; matrix products, arithmetic and copies ran while one was open for 25% of the time, Pallas kernels for 0%

commit v1 on v0

--- a/solution.py
+++ b/solution.py
@@ -301,7 +301,7 @@
         (zero_index, column_start),
     )
     norm_one_grad, norm_two_grad, router_grad, shared_gate_grad, bias_sum = lax.psum(
-        (norm_one_part, norm_two_part, router_part, gate_part, bias_full), ("dp", "tensor")
+        lax.psum((norm_one_part, norm_two_part, router_part, gate_part, bias_full), "tensor"), "dp"
     )
     qkv_bias_grad = lax.dynamic_slice(bias_sum, (zero_index, column_start), (3, qkv_cols))
     qkv_sum, out_sum, expert_in_sum, expert_out_sum, shared_in_sum, shared_out_sum = (

time: 1680 us -> 1650 us (0.982)
  waiting for transfers between devices: 922 us -> 889 us
    psum x1, waiting for transfers between devices: 121 us -> 0.02 us  [on_device(): lax.psum((norm_one_part, norm_two_part, router_part, gate_part, bias_full...]
    psum x0 -> x1, waiting for transfers between devices: none -> 49.7 us  [on_device(): lax.psum(lax.psum((norm_one_part, norm_two_part, router_part, gate_part,...]
    reduce_scatter x1, waiting for transfers between devices: 4.1 us -> 44.9 us  [on_device(): lax.psum_scatter(expert_out_grad.astype(jnp.bfloat16), 'dp', scatter_dime...]
    psum x1, blocking collectives: 42.1 us -> 15.3 us  [on_device(): lax.psum((norm_one_part, norm_two_part, router_part, gate_part, bias_full...]
    psum x0 -> x1, blocking collectives: none -> 26.5 us  [on_device(): lax.psum(lax.psum((norm_one_part, norm_two_part, router_part, gate_part,...]
    unnamed x390 -> x386, local copies, waits for them, and re-layouts: 66.5 us -> 65.7 us
  transfers between devices with their start and end apart: 15 -> 16, of which waited for: 14 -> 13; matrix products, arithmetic and copies ran while one was open for 25% -> 26% of each run, Pallas kernels for 0% -> 0%
where the time goes in v1:
time: 1650 us; the launch traced here: 1640 us
  waiting for transfers between devices  889 us (54%)
  matrix products  451 us (27%)
  local copies, waits for them, and re-layouts  147 us (9%)
  other arithmetic  92.1 us (6%)
  blocking collectives  41.8 us (3%)
  between operations  17.2 us (1%)
    reduce_scatter x1, waiting for transfers between devices, on_device(): lax.psum_scatter(expert_in_grad.astype(jnp.bfloat16), 'dp', scatter_dimen...  147 us
    reduce_scatter x1, waiting for transfers between devices, on_device(): lax.psum_scatter(jnp.dot(mixed, out_weight, preferred_element_type=jnp.fl...  142 us
    reduce_scatter x1, waiting for transfers between devices, on_device(): lax.psum_scatter(shared_in_grad.astype(jnp.bfloat16), 'dp', scatter_dimen...  87.5 us
    dot_general x9, matrix products, expert_backward(): jnp.einsum('nc,dc->nd', d_gate_up, in_flat, preferred_element_type=jnp.fl...  83.8 us
    dot_general x9, matrix products, expert_forward(): result = jnp.dot(inner_act, down_weight, preferred_element_type=jnp.float32)  79.7 us
    reduce_scatter x1, waiting for transfers between devices, on_device(): lax.psum_scatter(grad_one.astype(jnp.bfloat16), 'tensor', scatter_dimensi...  77.9 us
    reduce_scatter x1, waiting for transfers between devices, on_device(): lax.psum_scatter(combined.astype(jnp.bfloat16), 'tensor', scatter_dimensi...  77 us
    all_gather x1, waiting for transfers between devices, on_device(): lax.all_gather((unit_one * gain_one).astype(jnp.bfloat16), 'tensor', axis...  69.4 us
  transfers between devices with their start and end apart: 16, of which 13 were waited for; matrix products, arithmetic and copies ran while one was open for 26% of the time, Pallas kernels for 0%

profile of v1, /device:TPU:1, one launch (start us, length us, event | category | flops | bytes accessed | tf_op | source)
XLA Modules:
  0.0 1639.2 jit_solution(3153903049042194364)
XLA Ops:
  26.3 69.4 %all-gather.5.cloned.1.call-done = bf16[1024,2048]{1,0:T(8,128)(2,1)} async-done(((bf16[256,2048]{1,0:T(8,128)(2,1)}), bf16[1024,2048]{1,0:T(8,128)(2,1)}) %all-gather.5.cloned.1.call-update) | async-done | bytes 4194320 | tf_op jit(solution)/shard_map/all_gather | solution.py:106
  140.0 142.3 %reduce-scatter.11.cloned.1.call-done = f32[256,2048]{1,0:T(8,128)} async-done(((f32[1024,2048]{1,0:T(8,128)}), f32[256,2048]{1,0:T(8,128)}) %reduce-scatter.11.cloned.1.call-update) | async-done | bytes 2097168 | tf_op jit(solution)/shard_map/reduce_scatter | solution.py:155
  289.6 11.4 copy.161
  301.1 15.0 copy.107
  316.7 16.4 fusion.447
  333.2 37.0 %all-gather.7.cloned.1.call-done = bf16[1024,2048]{1,0:T(8,128)(2,1)} async-done(((bf16[256,2048]{1,0:T(8,128)(2,1)}), bf16[1024,2048]{1,0:T(8,128)(2,1)}) %all-gather.7.cloned.1.call-update) | async-done | bytes 4194320 | tf_op jit(solution)/shard_map/all_gather | solution.py:164
  417.0 34.5 %all-gather.9.cloned.1.call-done = bf16[1024,2048]{1,0:T(8,128)(2,1)} async-done(((bf16[256,2048]{1,0:T(8,128)(2,1)}), bf16[1024,2048]{1,0:T(8,128)(2,1)}) %all-gather.9.cloned.1.call-update) | async-done | bytes 4194320 | tf_op jit(solution)/shard_map/all_gather | solution.py:192
  471.7 17.7 %fusion.46 = f32[1024,2,1408]{2,0,1:T(8,128)S(1)} fusion(bf16[2,1408,2048]{2,1,0:T(8,128)(2,1)} %bitcast.918, bf16[1024,2048]{1,0:T(8,128)(2,1)} %all-gather.7.cloned.1.call-done), kind=kOutput, calls=%fused_computation.74 | convolution fusion | flops 11811160064 | bytes 27262976 | tf_op jit(solution)/shard_map/dot_general | solution.py:50
  595.6 12.7 multiply_bitcast_fusion.1
  608.4 38.0 %fusion.19 = f32[1024,2048]{1,0:T(8,128)} fusion(f32[1024,2048]{1,0:T(8,128)} %fusion.501, f32[1024,2048]{1,0:T(8,128)} %fusion.500, f32[1024,2048]{1,0:T(8,128)} %fusion.499, f32[1024,2048]{1,0:T(8,128)} %fusion.498, f32[1024,2048]{1,0:T(8,128)} %fusion.497, f32[1024,2048]{1,0:T(8,128)} %fusion.496, f32[1024,2048]{1,0:T(8,128)} %fusion.495, ...), kind=kOutput, calls=%fused_computation.32 | convolution fusion | flops 11837112320 | bytes 101199872 | tf_op jit(solution)/shard_map/nc,dc->nd/dot_general | solution.py:67
  697.2 29.5 %add_convert_fusion = bf16[1024,2048]{1,0:T(8,128)(2,1)} fusion(f32[1024,2048]{1,0:T(8,128)} %fusion.319, f32[1024,2048]{1,0:T(8,128)} %fusion.323, f32[1024,2048]{1,0:T(8,128)} %fusion.327, f32[1024,2048]{1,0:T(8,128)} %fusion.331, f32[1024,2048]{1,0:T(8,128)} %fusion.335, f32[1024,2048]{1,0:T(8,128)} %fusion.339, f32[1024,2048]{1,0:T(8,128)} %fusion.343, ...), kind=kOutput, calls=%fused_computation.36 | convolution fusion | flops 5943328768 | bytes 79990784 | tf_op jit(solution)/shard_map/dot_general | solution.py:54
  726.8 62.5 %reduce-scatter.15.cloned.1.call-done = f32[256,2048]{1,0:T(8,128)} async-done(((f32[1024,2048]{1,0:T(8,128)}), f32[256,2048]{1,0:T(8,128)}) %reduce-scatter.15.cloned.1.call-update) | async-done | bytes 2097168 | tf_op jit(solution)/shard_map/reduce_scatter | solution.py:229
  792.8 77.0 %reduce-scatter.13.cloned.1.call-done = bf16[256,2048]{1,0:T(8,128)(2,1)} async-done(((bf16[1024,2048]{1,0:T(8,128)(2,1)}), bf16[256,2048]{1,0:T(8,128)(2,1)}) %reduce-scatter.13.cloned.1.call-update) | async-done | bytes 1048592 | tf_op jit(solution)/shard_map/reduce_scatter | solution.py:187
  933.8 19.2 %convolution_convert_fusion = bf16[2048,2,1408]{2,0,1:T(8,128)(2,1)} fusion(bf16[1024,2,1408]{0,2,1:T(8,128)(2,1)} %copy.137, bf16[1024,2048]{1,0:T(8,128)(2,1)} %all-gather.7.cloned.1.call-done), kind=kOutput, calls=%fused_computation.12 | convolution fusion | flops 11816927232 | bytes 21495808 | tf_op jit(solution)/shard_map/nd,nc->dc/dot_general | solution.py:66
  1046.0 11.5 convolution_convert_fusion.2
  1100.4 44.9 %reduce-scatter.25.cloned.1.call-done = bf16[8,352,256]{2,1,0:T(8,128)(2,1)} async-done(((bf16[8,352,2048]{2,1,0:T(8,128)(2,1)}), bf16[8,352,256]{2,1,0:T(8,128)(2,1)}) %reduce-scatter.25.cloned.1.call-update) | async-done | bytes 1441808 | tf_op jit(solution)/shard_map/reduce_scatter | solution.py:317
  1148.6 87.5 %reduce-scatter.27.cloned.1.call-done = bf16[256,2,1408]{2,0,1:T(8,128)(2,1)} async-done(((bf16[2048,2,1408]{2,0,1:T(8,128)(2,1)}), bf16[256,2,1408]{2,0,1:T(8,128)(2,1)}) %reduce-scatter.27.cloned.1.call-update) | async-done | bytes 1441808 | tf_op jit(solution)/shard_map/reduce_scatter | solution.py:320
  1240.5 40.3 %reduce-scatter.21.cloned.1.call-done = bf16[512,256]{1,0:T(8,128)(2,1)} async-done(((bf16[512,2048]{1,0:T(8,128)(2,1)}), bf16[512,256]{1,0:T(8,128)(2,1)}) %reduce-scatter.21.cloned.1.call-update) | async-done | bytes 262160 | tf_op jit(solution)/shard_map/reduce_scatter | solution.py:311
  1282.6 77.9 %reduce-scatter.17.cloned.1.call-done = bf16[256,2048]{1,0:T(8,128)(2,1)} async-done(((bf16[1024,2048]{1,0:T(8,128)(2,1)}), bf16[256,2048]{1,0:T(8,128)(2,1)}) %reduce-scatter.17.cloned.1.call-update) | async-done | bytes 1048592 | tf_op jit(solution)/shard_map/reduce_scatter | solution.py:291
  1362.6 15.3 all-reduce.3
  1377.9 26.5 %all-reduce.2 = (f32[2048]{0:T(1024)}, f32[3,2048]{1,0:T(4,128)S(1)}, f32[2048]{0:T(1024)}, f32[2048]{0:T(1024)}) all-reduce(f32[2048]{0:T(1024)S(1)} %get-tuple-element.124, f32[3,2048]{1,0:T(4,128)S(1)} %get-tuple-element.125, f32[2048]{0:T(1024)S(1)} %get-tuple-element.126, ...), channel_id=1, replica_groups=mesh['dp'=8,'tensor'=4] {'dp'}, use_global_device_ids=true, to_apply=%region_29.30 | all-reduce | flops 12288 | bytes 98304 | tf_op jit(solution)/shard_map/psum | solution.py:303
  1408.9 18.0 %reduce-scatter.19.cloned.1.call-done = bf16[256,3,512]{2,0,1:T(8,128)(2,1)} async-done(((bf16[2048,3,512]{2,0,1:T(8,128)(2,1)}), bf16[256,3,512]{2,0,1:T(8,128)(2,1)}) %reduce-scatter.19.cloned.1.call-update) | async-done | bytes 786448 | tf_op jit(solution)/shard_map/reduce_scatter | solution.py:308
  1429.3 146.9 %reduce-scatter.23.cloned.1.call-done = bf16[8,256,2,352]{1,3,2,0:T(8,128)(2,1)} async-done(((bf16[8,2048,2,352]{1,3,2,0:T(8,128)(2,1)}), bf16[8,256,2,352]{1,3,2,0:T(8,128)(2,1)}) %reduce-scatter.23.cloned.1.call-update) | async-done | bytes 2883600 | tf_op jit(solution)/shard_map/reduce_scatter | solution.py:314
  1581.2 49.7 %all-reduce.9.cloned.1.call-done = f32[2048,8]{0,1:T(8,128)} async-done(((f32[2048,8]{0,1:T(8,128)}), f32[2048,8]{0,1:T(8,128)}) %all-reduce.9.cloned.1.call-update) | async-done | bytes 65552 | tf_op jit(solution)/shard_map/psum | solution.py:303
  (604 shorter events, 520.7 us)
Async XLA Ops:
  7.2 88.5 %all-gather.5.cloned.1.call-start = ((), (), s32[]{:S(2)}) async-start(), calls=%async_computation.10 | async-start | bytes 5242880 | tf_op jit(solution)/shard_map/all_gather | solution.py:106
  12.7 269.6 %reduce-scatter.11.cloned.1.call-start = ((), (), s32[]{:S(2)}) async-start(), calls=%async_computation.11 | async-start | bytes 10485760 | tf_op jit(solution)/shard_map/reduce_scatter | solution.py:155
  139.3 230.9 %all-gather.7.cloned.1.call-start = ((), (), s32[]{:S(2)}) async-start(), calls=%async_computation.12 | async-start | bytes 5242880 | tf_op jit(solution)/shard_map/all_gather | solution.py:164
  140.0 145.9 %copy-start.129 = (f32[2048]{0:T(1024)}, f32[2048]{0:T(1024)S(1)}, u32[]{:S(2)}) copy-start(f32[2048]{0:T(1024)S(1)} %convert_element_type.408) | copy-start | bytes 24580
  140.0 145.8 %copy-start.162 = (f32[256]{0:T(256)}, f32[256]{0:T(256)S(1)}, u32[]{:S(2)}) copy-start(f32[256]{0:T(256)S(1)} %compare_convert_fusion) | copy-start | bytes 3076
  288.3 163.2 %all-gather.9.cloned.1.call-start = ((), (), s32[]{:S(2)}) async-start(), calls=%async_computation.14 | async-start | bytes 5242880 | tf_op jit(solution)/shard_map/all_gather | solution.py:192
  333.1 456.2 %reduce-scatter.15.cloned.1.call-start = ((), (), s32[]{:S(2)}) async-start(), calls=%async_computation.15 | async-start | bytes 10485760 | tf_op jit(solution)/shard_map/reduce_scatter | solution.py:229
  646.4 223.4 %reduce-scatter.13.cloned.1.call-start = ((), (), s32[]{:S(2)}) async-start(), calls=%async_computation.13 | async-start | bytes 5242880 | tf_op jit(solution)/shard_map/reduce_scatter | solution.py:187
  726.8 143.0 %copy-start.28 = (bf16[256,2048]{1,0:T(8,128)(2,1)S(1)}, bf16[256,2048]{1,0:T(8,128)(2,1)}, u32[]{:S(2)}) copy-start(bf16[256,2048]{1,0:T(8,128)(2,1)} %param.30) | copy-start | bytes 3145732
  726.8 232.1 %all-gather.11.cloned.1.call-start = ((), (), s32[]{:S(2)}) async-start(), calls=%async_computation.16 | async-start | bytes 5242880 | tf_op jit(solution)/shard_map/all_gather | solution.py:232
  875.6 222.0 %all-reduce.7.cloned.1.call-start = ((), (), s32[]{:S(2)}) async-start(), calls=%async_computation.20 | async-start | bytes 131072 | tf_op jit(solution)/shard_map/psum | solution.py:304
  880.9 217.2 %reduce-scatter.29.cloned.1.call-start = ((), (), s32[]{:S(2)}) async-start(), calls=%async_computation.25 | async-start | bytes 6488064 | tf_op jit(solution)/shard_map/reduce_scatter | solution.py:323
  891.8 253.5 %reduce-scatter.25.cloned.1.call-start = ((), (), s32[]{:S(2)}) async-start(), calls=%async_computation.23 | async-start | bytes 12976128 | tf_op jit(solution)/shard_map/reduce_scatter | solution.py:317
  919.1 316.9 %reduce-scatter.27.cloned.1.call-start = ((), (), s32[]{:S(2)}) async-start(), calls=%async_computation.24 | async-start | bytes 12976128 | tf_op jit(solution)/shard_map/reduce_scatter | solution.py:320
  953.0 327.8 %reduce-scatter.21.cloned.1.call-start = ((), (), s32[]{:S(2)}) async-start(), calls=%async_computation.19 | async-start | bytes 2359296 | tf_op jit(solution)/shard_map/reduce_scatter | solution.py:311
  990.3 370.2 %reduce-scatter.17.cloned.1.call-start = ((), (), s32[]{:S(2)}) async-start(), calls=%async_computation.17 | async-start | bytes 5242880 | tf_op jit(solution)/shard_map/reduce_scatter | solution.py:291
  1041.0 385.8 %reduce-scatter.19.cloned.1.call-start = ((), (), s32[]{:S(2)}) async-start(), calls=%async_computation.18 | async-start | bytes 7077888 | tf_op jit(solution)/shard_map/reduce_scatter | solution.py:308
  1057.5 518.7 %reduce-scatter.23.cloned.1.call-start = ((), (), s32[]{:S(2)}) async-start(), calls=%async_computation.22 | async-start | bytes 25952256 | tf_op jit(solution)/shard_map/reduce_scatter | solution.py:314
  1097.5 533.4 %all-reduce.9.cloned.1.call-start = ((), (), s32[]{:S(2)}) async-start(), calls=%async_computation.21 | async-start | bytes 131072 | tf_op jit(solution)/shard_map/psum | solution.py:303
  1148.5 212.0 %copy-start.11 = (bf16[256,2048]{1,0:T(8,128)(2,1)S(1)}, bf16[256,2048]{1,0:T(8,128)(2,1)}, u32[]{:S(2)}) copy-start(bf16[256,2048]{1,0:T(8,128)(2,1)} %param.27) | copy-start | bytes 3145732
  1148.5 212.0 %copy-start.127 = (f32[2048]{0:T(1024)S(1)}, f32[2048]{0:T(1024)}, u32[]{:S(2)}) copy-start(f32[2048]{0:T(1024)} %copy-done.126) | copy-start | bytes 24580
  1148.5 212.0 %copy-start.157 = (f32[256]{0:T(256)S(1)}, f32[256]{0:T(256)}, u32[]{:S(2)}) copy-start(f32[256]{0:T(256)} %copy-done.156) | copy-start | bytes 3076
  1148.5 214.0 %slice-start.10 = ((f32[9,2048]{1,0:T(8,128)}), f32[1,2048]{1,0:T(1,128)S(1)}, s32[]{:S(2)}) async-start(f32[9,2048]{1,0:T(8,128)} %copy-done.123), calls=%async_computation.36 | async-start | bytes 16384 | tf_op jit(solution)/shard_map/slice | solution.py:228
  1148.6 214.0 %copy-start.152 = (f32[2048]{0:T(1024)S(1)}, f32[2048]{0:T(1024)}, u32[]{:S(2)}) copy-start(f32[2048]{0:T(1024)} %get-tuple-element.116) | copy-start | bytes 24580
  (183 other events, 2207.2 us)
Sparse Core Ops, SparseCore 0:
  12.8 82.8 all-gather.4
  139.4 142.8 reduce-scatter.10
  288.5 81.6 all-gather.6
  372.2 79.2 all-gather.8
  646.5 142.8 reduce-scatter.14
  792.1 77.6 reduce-scatter.12
  875.7 81.2 all-gather.10
  960.0 30.5 all-reduce.6
  994.0 60.7 reduce-scatter.28
  1058.5 86.7 reduce-scatter.24
  1149.2 86.7 reduce-scatter.26
  1239.5 41.2 reduce-scatter.20
  1283.7 76.7 reduce-scatter.16
  1364.1 62.6 reduce-scatter.18
  1430.3 145.8 reduce-scatter.22
  1579.2 51.7 all-reduce.8
